TPU v7x, 256 devices: a whole 4x4x8 slice. The times are simulated.
256 devices in a mesh: dp: 8 (over z), own: 32 (over x, y, core).
Axes of the slice: x: 4, y: 4, z: 8, core: 2. Of those that a mesh axis runs over, the one named last changes fastest.
Arguments:
- signals: bfloat16 [65536, 384], P(('dp', 'own')), may hold values from -6 to 6
- cotangent: bfloat16 [65536, 384], P(('dp', 'own')), may hold values from -6 to 6
- row_insertion: int32 [65536], P(('dp', 'own')), may hold values from 0 to 63, as said below
- touched: int32 [256, 4], replicated, may hold values from 0 to 63, as said below
- slot_map: int32 [64], replicated, may hold values from 0 to 63, each once
- weights: bfloat16 [64, 2, 384, 1024], P(None, None, 'own'), may hold values from -0.3125 to 0.3125
- moment1: float32 [64, 2, 384, 1024], P(None, None, 'own', 'dp'), may hold values from -25.6 to 25.6
- moment2: float32 [64, 2, 384, 1024], P(None, None, 'own', 'dp'), may hold values from 0.2048 to 6.144
Outputs:
- predicted: bfloat16 [65536, 384], P(('dp', 'own'))
- new_weights: bfloat16 [64, 2, 384, 1024], P(None, None, 'own')
- new_moment1: float32 [64, 2, 384, 1024], P(None, None, 'own', 'dp')
- new_moment2: float32 [64, 2, 384, 1024], P(None, None, 'own', 'dp')
Inputs may be any that keep to these rules, and one draw needn't show every extreme that they name: `row_insertion`: device d (dp index times the size of own plus own index) holds rows d * 256 to (d + 1) * 256 - 1; their insertions are all in row d of touched; at most 128 rows of one device name the same insertion, and on every device one insertion is named by exactly 128 rows. `touched`: each row lists 4 different insertions.
All inputs are finite; a program needn't handle non-finite values.
Results may differ from a plain program's by a relative error of at most 0.0049.
Values may be sent and summed in bfloat16 or wider, within the bound.
A program may use at most 128 MiB of HBM per device.

v0:
```python
import math
import jax
import jax.numpy as jnp
from jax import lax
from jax.sharding import PartitionSpec as P

SITES = 384
WIDTH = 1024
TOUCH = 4
CAP = 128
gelu_coef = math.sqrt(2.0 / math.pi)
cubic_coef = 0.044715
learn_rate = 0.01
highest = lax.Precision.HIGHEST


def gelu_parts(preact):
    tanh_input = gelu_coef * (preact + cubic_coef * preact * preact * preact)
    tangent = jnp.tanh(tanh_input)
    gelu_val = 0.5 * preact * (1.0 + tangent)
    slopes = 0.5 * (1.0 + tangent) + 0.5 * preact * (1.0 - tangent * tangent) * gelu_coef * (
        1.0 + 3.0 * cubic_coef * preact * preact
    )
    return (gelu_val, slopes)


def dispatch(row_ids, listed):
    match_table = (row_ids[:, None] == listed[None, :]).astype(jnp.int32)
    running = jnp.cumsum(match_table, axis=0) - 1
    slot_of = jnp.sum(match_table * jnp.arange(listed.shape[0], dtype=jnp.int32)[None, :], axis=1)
    within = jnp.sum(match_table * running, axis=1)
    return slot_of * CAP + within


def adam_step(params, moment_one, moment_two, gradient):
    moment_one = 0.9 * moment_one + 0.1 * gradient
    moment_two = 0.999 * moment_two + 0.001 * gradient * gradient
    correct_one = 1.0 - 0.9**10
    correct_two = 1.0 - 0.999**10
    updated = params - learn_rate * (moment_one / correct_one) / (
        jnp.sqrt(moment_two / correct_two) + 1e-08
    )
    return (updated.astype(jnp.bfloat16), moment_one, moment_two)


def sum_by_insertion(item_rows, arrived_grad, number):
    one_hot = (jnp.arange(number, dtype=jnp.int32)[:, None] == item_rows[None, :]).astype(
        arrived_grad.dtype
    )
    flat_grad = arrived_grad.reshape(item_rows.shape[0], -1)
    return jnp.dot(one_hot, flat_grad, preferred_element_type=jnp.float32)


def shards(signals, cotangent, row_insertion, touched, slot_map, weights, moment1, moment2):
    n_own = lax.axis_size("own")
    n_dp = lax.axis_size("dp")
    dp_at = lax.axis_index("dp")
    own_at = lax.axis_index("own")
    number = weights.shape[0]
    piece_rows = weights.shape[2]
    width_part = moment1.shape[3]
    stored = jnp.sum(
        jnp.where(
            touched[:, :, None] == jnp.arange(number, dtype=jnp.int32)[None, None, :],
            slot_map[None, None, :],
            0,
        ),
        axis=2,
    )
    stored_all = stored.reshape(n_dp, n_own, TOUCH)
    group_rows = lax.dynamic_index_in_dim(stored_all, dp_at, 0, keepdims=False)
    flat_rows = group_rows.reshape(-1)
    my_list = lax.dynamic_index_in_dim(touched, dp_at * n_own + own_at, 0, keepdims=False)
    places = dispatch(row_insertion, my_list)
    stacked = (
        jnp.zeros((TOUCH * CAP, 2 * SITES), signals.dtype)
        .at[places]
        .set(jnp.concatenate([signals, cotangent], axis=1))
    )
    stacked = stacked.reshape(TOUCH, CAP, 2 * SITES)
    sig_slots = stacked[:, :, :SITES]
    cot_slots = stacked[:, :, SITES:]
    read_out = None
    outgoing = jnp.take(weights, flat_rows, axis=0).reshape(n_own, TOUCH, 2, piece_rows, WIDTH)
    arrived = lax.all_to_all(outgoing, "own", split_axis=0, concat_axis=3, tiled=True)
    read_in = arrived[0, :, 0]
    read_out = arrived[0, :, 1]
    preact = jnp.einsum("kcs,ksw->kcw", sig_slots, read_in, preferred_element_type=jnp.float32)
    gelu_val, slopes = gelu_parts(preact)
    hidden = gelu_val.astype(jnp.bfloat16)
    pred_slots = jnp.einsum(
        "kcw,ksw->kcs", hidden, read_out, preferred_element_type=jnp.float32
    ).astype(jnp.bfloat16)
    back_hidden = jnp.einsum(
        "kcs,ksw->kcw", cot_slots, read_out, preferred_element_type=jnp.float32
    )
    back_pre = (back_hidden * slopes).astype(jnp.bfloat16)
    grad_in = jnp.einsum("kcs,kcw->ksw", sig_slots, back_pre, preferred_element_type=jnp.float32)
    grad_out = jnp.einsum("kcs,kcw->ksw", cot_slots, hidden, preferred_element_type=jnp.float32)
    grads = jnp.stack([grad_in, grad_out], axis=1).astype(jnp.bfloat16)
    arrived_grad = lax.all_to_all(
        lax.all_to_all(grads[None, None], "dp", split_axis=5, concat_axis=0, tiled=True),
        "own",
        split_axis=4,
        concat_axis=1,
        tiled=True,
    )
    table = sum_by_insertion(stored.reshape(-1), arrived_grad, number).reshape(
        number, 2, piece_rows, width_part
    )
    own_params = lax.dynamic_slice_in_dim(weights, dp_at * width_part, width_part, 3).astype(
        jnp.float32
    )
    fresh_part, new_moment1, new_moment2 = adam_step(own_params, moment1, moment2, table)
    new_weights = lax.all_gather(fresh_part, "dp", axis=3, tiled=True)
    predicted = pred_slots.reshape(TOUCH * CAP, SITES)[places]
    return (predicted, new_weights, new_moment1, new_moment2)


def solution(mesh):
    in_specs = (
        P(("dp", "own"), None),
        P(("dp", "own"), None),
        P(("dp", "own")),
        P(),
        P(),
        P(None, None, "own", None),
        P(None, None, "own", "dp"),
        P(None, None, "own", "dp"),
    )
    out_specs = (
        P(("dp", "own"), None),
        P(None, None, "own", None),
        P(None, None, "own", "dp"),
        P(None, None, "own", "dp"),
    )
    return jax.shard_map(shards, mesh=mesh, in_specs=in_specs, out_specs=out_specs, check_vma=False)
```

profile of v0, /device:TPU:32, one launch (start us, length us, event | category | flops | bytes accessed | tf_op | source)
XLA Modules:
  0.0 529.9 jit_solution(10570098943533189898)
XLA Ops:
  7.2 0.0 copy-start
  7.2 1.0 select_reduce_fusion
  8.1 0.1 copy.106
  8.3 0.1 reshape.153
  8.4 0.1 copy.84
  8.5 0.1 copy.85
  8.6 0.5 copy-done
  9.1 16.2 %gather_fusion = bf16[128,2,12,1024]{3,1,2,0:T(2,128)(2,1)} fusion(bf16[64,2,12,1024]{3,1,2,0:T(2,128)(2,1)S(1)} %copy-done, s32[1024]{0:T(1024)S(1)} %pad_clamp_fusion.1), kind=kCustom, calls=%fused_computation | custom fusion | bytes 12583424 | tf_op jit(solution)/shard_map/jit(_take)/gather | solution.py:84
  25.3 8.9 %broadcast_select_fusion = bf16[32,4,2,12,1024]{4,2,3,1,0:T(2,128)(2,1)} fusion(bf16[32,4,2,12,1024]{4,2,3,1,0:T(2,128)(2,1)} %bitcast.61, pred[32,4]{1,0:T(8,128)(4,1)S(1)} %copy.85), kind=kLoop, calls=%fused_computation.3 | loop fusion | flops 3145728 | bytes 12583040 | tf_op jit(solution)/shard_map/jit(_take)/select_n | solution.py:84
  34.2 0.0 copy-start.5
  34.2 0.0 copy-start.6
  34.2 0.0 copy-start.4
  34.2 7.6 %all-to-all-start = ((bf16[32,4,2,12,1024]{4,2,3,1,0:T(2,128)(2,1)}), bf16[32,4,2,12,1024]{4,2,3,1,0:T(2,128)(2,1)}, u32[]{:S(2)}, u32[]{:S(2)}) async-start(bf16[32,4,2,12,1024]{4,2,3,1,0:T(2,128)(2,1)} %broadcast_select_fusion), calls=%async_computation | async-start | bytes 12582912 | tf_op jit(solution)/shard_map/all_to_all | solution.py:85
  41.8 0.0 copy-done.5
  41.8 0.2 dynamic-slice_reduce_fusion
  42.0 0.0 copy-done.6
  42.0 0.1 compare_convert_fusion
  42.1 1.2 reduce-window.6
  43.3 0.1 slice.28
  43.4 0.1 copy.81
  43.5 0.1 copy.82
  43.6 0.1 add_bitcast_fusion
  43.7 0.1 fusion.24
  43.8 0.0 copy-done.4
  43.8 3.0 scatter_custom_fusion
  46.8 74.9 %all-to-all-done = bf16[32,4,2,12,1024]{4,2,3,1,0:T(2,128)(2,1)} async-done(((bf16[32,4,2,12,1024]{4,2,3,1,0:T(2,128)(2,1)}), bf16[32,4,2,12,1024]{4,2,3,1,0:T(2,128)(2,1)}, u32[]{:S(2)}, u32[]{:S(2)}) %all-to-all-start) | async-done | bytes 6291488 | tf_op jit(solution)/shard_map/all_to_all | solution.py:85
  121.7 6.4 %copy.86 = bf16[1,4,2,32,12,1024]{5,2,4,3,1,0:T(2,128)(2,1)S(1)} copy(bf16[1,4,2,32,12,1024]{5,2,4,1,3,0:T(2,128)(2,1)} %bitcast.11) | data formatting | bytes 12582912 | tf_op jit(solution)/shard_map/all_to_all | solution.py:85
  128.1 0.0 copy-start.3
  128.1 9.8 %fusion.34 = (bf16[1,4,1,384,1024]{4,2,3,1,0:T(2,128)(2,1)S(1)}, bf16[1,4,1,384,1024]{4,2,3,1,0:T(2,128)(2,1)}) fusion(bf16[1,4,2,384,1024]{4,2,3,1,0:T(2,128)(2,1)S(1)} %bitcast.60), kind=kLoop, calls=%fused_computation.65 | loop fusion | bytes 12582912 | tf_op jit(solution)/shard_map/slice | solution.py:86
  137.9 0.0 copy-done.3
  137.9 1.2 fusion
  139.1 0.0 copy-start.2
  139.1 2.7 convert_bitcast_fusion
  141.9 0.0 copy-done.2
  141.9 8.3 %convert_bitcast_fusion.1 = bf16[1,1,4,1,384,1024]{5,4,2,3,1,0:T(8,128)(2,1)} fusion(f32[4,128,1024]{2,1,0:T(8,128)} %copy-done.2, bf16[1,4,1,384,1024]{4,2,3,1,0:T(2,128)(2,1)} %get-tuple-element.30, bf16[4,128,768]{2,1,0:T(8,128)(2,1)} %bitcast.68), kind=kOutput, calls=%fused_computation.9 | convolution fusion | flops 816840704 | bytes 9175040 | tf_op jit(solution)/shard_map/kcs,kcw->ksw/dot_general | solution.py:98
  150.2 6.1 %pad_maximum_fusion = bf16[1,1,4,2,384,1024]{5,4,2,3,1,0:T(8,128)(2,1)} fusion(bf16[1,1,4,1,384,1024]{5,4,2,3,1,0:T(8,128)(2,1)} %convert_bitcast_fusion, bf16[1,1,4,1,384,1024]{5,4,2,3,1,0:T(8,128)(2,1)} %convert_bitcast_fusion.1), kind=kLoop, calls=%fused_computation.4 | loop fusion | flops 3145728 | bytes 12582912 | tf_op jit(solution)/shard_map/stack | solution.py:100
  156.3 10.9 %copy.94 = bf16[1,1,4,2,384,1024]{4,2,3,1,0,5:T(4,128)(2,1)} copy(bf16[1,1,4,2,384,1024]{5,4,2,3,1,0:T(8,128)(2,1)} %pad_maximum_fusion) | data formatting | bytes 12582912 | tf_op jit(solution)/shard_map/stack | solution.py:100
  167.1 146.8 %all_to_all.51 = bf16[1,1,4,2,384,1024]{4,2,3,1,0,5:T(4,128)(2,1)} all-to-all(bf16[1,1,4,2,384,1024]{4,2,3,1,0,5:T(4,128)(2,1)} %copy.94), channel_id=1, replica_groups=mesh['dp'=8,'own'=32] {'dp'}, dimensions={5} | all-to-all | bytes 12582912 | tf_op jit(solution)/shard_map/all_to_all | solution.py:102
  313.9 12.3 %copy.95 = bf16[1,1,4,2,384,8,128]{6,5,3,2,4,1,0:T(8,128)(2,1)} copy(bf16[1,1,4,2,384,8,128]{4,2,3,6,5,1,0:T(4,128)(2,1)} %bitcast.64) | data formatting | bytes 12582912 | tf_op jit(solution)/shard_map/all_to_all | solution.py:102
  326.3 14.0 %all-to-all-start.2 = ((bf16[8,1,4,2,384,128]{5,0,3,2,1,4:T(8,128)(2,1)}), bf16[8,1,4,2,384,128]{5,0,3,2,1,4:T(8,128)(2,1)}, u32[]{:S(2)}, u32[]{:S(2)}) async-start(bf16[8,1,4,2,384,128]{5,0,3,2,1,4:T(8,128)(2,1)} %bitcast.62), calls=%async_computation.2 | async-start | bytes 12582912 | tf_op jit(solution)/shard_map/all_to_all | solution.py:101
  340.3 0.0 all-gather.2.cloned.1.call-start
  340.3 0.1 eq.65
  340.5 0.3 constant_dynamic-slice_fusion.1
  340.8 79.3 %all-to-all-done.2 = bf16[8,1,4,2,384,128]{5,0,3,2,1,4:T(8,128)(2,1)} async-done(((bf16[8,1,4,2,384,128]{5,0,3,2,1,4:T(8,128)(2,1)}), bf16[8,1,4,2,384,128]{5,0,3,2,1,4:T(8,128)(2,1)}, u32[]{:S(2)}, u32[]{:S(2)}) %all-to-all-start.2) | async-done | bytes 6291488 | tf_op jit(solution)/shard_map/all_to_all | solution.py:101
  420.1 3.9 copy.96
  424.1 5.6 %copy.97 = bf16[8,32,1,4,2,12,128]{6,5,4,3,1,0,2:T(8,128)(2,1)} copy(bf16[8,32,1,4,2,12,128]{6,0,5,1,4,3,2:T(8,128)(2,1)S(1)} %bitcast.65) | data formatting | bytes 12582912 | tf_op jit(solution)/shard_map/all_to_all | solution.py:101
  429.7 12.1 %reshape.155 = bf16[1024,3072]{1,0:T(8,128)(2,1)} reshape(bf16[8,32,1,4,2,12,128]{6,5,4,3,1,0,2:T(8,128)(2,1)} %copy.97) | data formatting | bytes 12582912 | tf_op jit(solution)/shard_map/reshape | solution.py:50
  441.7 8.7 %copy.98 = bf16[3072,1024]{1,0:T(8,128)(2,1)} copy(bf16[3072,1024]{0,1:T(8,128)(2,1)} %bitcast.66) | data formatting | bytes 12582912 | tf_op jit(solution)/shard_map/dot_general | solution.py:51
  450.4 7.0 %subtract_convert_fusion = (bf16[64,2,12,128]{3,0,2,1:T(8,128)(2,1)}, f32[64,2,12,128]{3,0,2,1:T(8,128)}, f32[64,2,12,128]{3,0,2,1:T(8,128)}) fusion(bf16[64,2,12,128]{3,1,2,0:T(2,128)(2,1)S(1)} %constant_dynamic-slice_fusion.1, f32[64,2,12,128]{3,1,2,0:T(2,128)} %param.14, f32[64,2,12,128]{3,1,2,0:T(2,128)} %param.15, ...), kind=kOutput, calls=%fused_computation.26 | convolution fusion | flops 405471232 | bytes 10227712 | tf_op jit(solution)/shard_map/dot_general | solution.py:51
  457.4 0.0 all-gather.2.cloned.1.call-update
  457.4 4.9 convolution_convert_fusion
  462.4 1.8 gather_fusion.1
  464.2 0.0 copy-start.1
  464.2 2.7 copy.101
  466.9 0.0 copy-done.1
  466.9 1.5 copy.102
  468.4 47.9 %all-gather.2.cloned.1.call-done = bf16[64,2,12,1024]{3,0,2,1:T(8,128)(2,1)} async-done(((bf16[64,2,12,128]{3,0,2,1:T(8,128)(2,1)}), bf16[64,2,12,1024]{3,0,2,1:T(8,128)(2,1)}) %all-gather.2.cloned.1.call-update) | async-done | bytes 3145744 | tf_op jit(solution)/shard_map/all_gather | solution.py:115
  516.3 6.8 %copy.100 = bf16[64,2,12,1024]{3,1,2,0:T(2,128)(2,1)} copy(bf16[64,2,12,1024]{3,0,2,1:T(8,128)(2,1)} %all-gather.2.cloned.1.call-done) | data formatting | bytes 6291456
  (9 shorter events, 0.1 us)
Async XLA Ops:
  7.2 1.9 copy-start
  34.2 7.6 %copy-start.5 = (s32[256,4]{0,1:T(4,128)S(1)}, s32[256,4]{0,1:T(4,128)}, u32[]{:S(2)}) copy-start(s32[256,4]{0,1:T(4,128)} %param.11) | copy-start | bytes 12292
  34.2 7.8 %copy-start.6 = (s32[256]{0:T(256)S(1)}, s32[256]{0:T(256)}, u32[]{:S(2)}) copy-start(s32[256]{0:T(256)} %param.10) | copy-start | bytes 3076
  34.2 9.6 %copy-start.4 = (bf16[256,384]{1,0:T(8,128)(2,1)S(1)}, bf16[256,384]{1,0:T(8,128)(2,1)}, u32[]{:S(2)}) copy-start(bf16[256,384]{1,0:T(8,128)(2,1)} %param.9) | copy-start | bytes 589828
  34.2 87.4 %all-to-all-start = ((bf16[32,4,2,12,1024]{4,2,3,1,0:T(2,128)(2,1)}), bf16[32,4,2,12,1024]{4,2,3,1,0:T(2,128)(2,1)}, u32[]{:S(2)}, u32[]{:S(2)}) async-start(bf16[32,4,2,12,1024]{4,2,3,1,0:T(2,128)(2,1)} %broadcast_select_fusion), calls=%async_computation | async-start | bytes 12582912 | tf_op jit(solution)/shard_map/all_to_all | solution.py:85
  128.1 9.8 %copy-start.3 = (bf16[512,768]{1,0:T(8,128)(2,1)S(1)}, bf16[512,768]{1,0:T(8,128)(2,1)}, u32[]{:S(2)}) copy-start(bf16[512,768]{1,0:T(8,128)(2,1)} %scatter_custom_fusion) | copy-start | bytes 2359300
  139.1 2.7 copy-start.2
  326.3 93.9 %all-to-all-start.2 = ((bf16[8,1,4,2,384,128]{5,0,3,2,1,4:T(8,128)(2,1)}), bf16[8,1,4,2,384,128]{5,0,3,2,1,4:T(8,128)(2,1)}, u32[]{:S(2)}, u32[]{:S(2)}) async-start(bf16[8,1,4,2,384,128]{5,0,3,2,1,4:T(8,128)(2,1)} %bitcast.62), calls=%async_computation.2 | async-start | bytes 12582912 | tf_op jit(solution)/shard_map/all_to_all | solution.py:101
  340.3 176.0 %all-gather.2.cloned.1.call-start = ((), (), s32[]{:S(2)}) async-start(), calls=%async_computation.3 | async-start | bytes 3538944 | tf_op jit(solution)/shard_map/all_gather | solution.py:115
  464.2 2.7 copy-start.1
Sparse Core Ops, SparseCore 0:
  457.5 58.6 all-gather.1
where the time goes:
time: 531 us; the launch traced here: 530 us
  waiting for transfers between devices  202 us (38%)
  blocking collectives  147 us (28%)
  local copies, waits for them, and re-layouts  100 us (19%)
  matrix products  24.2 us (5%)
  starting transfers between devices  21.6 us (4%)
  other arithmetic  20.5 us (4%)
  between operations  14.2 us (3%)
    all_to_all x1, blocking collectives, shards(): lax.all_to_all(grads[None, None], 'dp', split_axis=5, concat_axis=0, tile...  147 us
    all_to_all x1, waiting for transfers between devices, shards(): lax.all_to_all(lax.all_to_all(grads[None, None], 'dp', split_axis=5, conc...  79.3 us
    all_to_all x1, waiting for transfers between devices, shards(): lax.all_to_all(outgoing, 'own', split_axis=0, concat_axis=3, tiled=True)  74.9 us
    all_gather x1, waiting for transfers between devices, shards(): new_weights = lax.all_gather(fresh_part, 'dp', axis=3, tiled=True)  47.9 us
    gather x1, local copies, waits for them, and re-layouts, shards(): jnp.take(weights, flat_rows, axis=0)  16.2 us
    all_to_all x1, starting transfers between devices, shards(): lax.all_to_all(lax.all_to_all(grads[None, None], 'dp', split_axis=5, conc...  14 us
    all_to_all x1, local copies, waits for them, and re-layouts, shards(): lax.all_to_all(grads[None, None], 'dp', split_axis=5, concat_axis=0, tile...  12.3 us
    reshape x1, local copies, waits for them, and re-layouts, sum_by_insertion(): flat_grad = arrived_grad.reshape(item_rows.shape[0], -1)  12.1 us
  transfers between devices with their start and end apart: 3, of which 3 were waited for; matrix products, arithmetic and copies ran while one was open for 3% of the time, Pallas kernels for 0%

commit v1 on v0

--- a/solution.py
+++ b/solution.py
@@ -112,7 +112,8 @@
         jnp.float32
     )
     fresh_part, new_moment1, new_moment2 = adam_step(own_params, moment1, moment2, table)
-    new_weights = lax.all_gather(fresh_part, "dp", axis=3, tiled=True)
+    copies = jnp.concatenate([fresh_part] * lax.axis_size("dp"), axis=3)
+    new_weights = lax.all_to_all(copies, "dp", 3, 3, tiled=True)
     predicted = pred_slots.reshape(TOUCH * CAP, SITES)[places]
     return (predicted, new_weights, new_moment1, new_moment2)
 

time: 531 us -> 594 us (1.12)
  the two profiles are of different devices: /device:TPU:32 before, /device:TPU:8 now
where the time goes in v1:
time: 594 us; the launch traced here: 592 us
  waiting for transfers between devices  232 us (39%)
  local copies, waits for them, and re-layouts  149 us (25%)
  blocking collectives  149 us (25%)
  matrix products  23.8 us (4%)
  other arithmetic  20.5 us (3%)
  starting transfers between devices  16.4 us (3%)
    all_to_all x1, blocking collectives, shards(): lax.all_to_all(grads[None, None], 'dp', split_axis=5, concat_axis=0, tile...  149 us
    all_to_all x1, waiting for transfers between devices, shards(): lax.all_to_all(lax.all_to_all(grads[None, None], 'dp', split_axis=5, conc...  87.5 us
    all_to_all x1, waiting for transfers between devices, shards(): lax.all_to_all(outgoing, 'own', split_axis=0, concat_axis=3, tiled=True)  82.6 us
    all_to_all x1, waiting for transfers between devices, shards(): new_weights = lax.all_to_all(copies, 'dp', 3, 3, tiled=True)  61.7 us
    unnamed x29, local copies, waits for them, and re-layouts  43.1 us
    concatenate x2, local copies, waits for them, and re-layouts, shards(): copies = jnp.concatenate([fresh_part] * lax.axis_size('dp'), axis=3)  16.7 us
    gather x1, local copies, waits for them, and re-layouts, shards(): jnp.take(weights, flat_rows, axis=0)  16.2 us
    all_to_all x1, local copies, waits for them, and re-layouts, shards(): lax.all_to_all(grads[None, None], 'dp', split_axis=5, concat_axis=0, tile...  12.3 us
  transfers between devices with their start and end apart: 3, of which 3 were waited for; matrix products, arithmetic and copies ran while one was open for 3% of the time, Pallas kernels for 0%

profile of v1, /device:TPU:8, one launch (start us, length us, event | category | flops | bytes accessed | tf_op | source)
XLA Modules:
  0.0 591.6 jit_solution(17152235068241210340)
XLA Ops:
  0.6 0.0 copy-start
  0.7 1.0 select_reduce_fusion
  1.6 0.1 copy.130
  1.8 0.1 reshape.153
  1.9 0.1 copy.107
  2.0 0.1 copy.108
  2.1 0.5 copy-done
  2.6 16.2 %gather_fusion = bf16[128,2,12,1024]{3,1,2,0:T(2,128)(2,1)} fusion(bf16[64,2,12,1024]{3,1,2,0:T(2,128)(2,1)S(1)} %copy-done, s32[1024]{0:T(1024)S(1)} %pad_clamp_fusion.1), kind=kCustom, calls=%fused_computation | custom fusion | bytes 12583424 | tf_op jit(solution)/shard_map/jit(_take)/gather | solution.py:84
  18.8 8.9 %broadcast_select_fusion = bf16[32,4,2,12,1024]{4,2,3,1,0:T(2,128)(2,1)} fusion(bf16[32,4,2,12,1024]{4,2,3,1,0:T(2,128)(2,1)} %bitcast.63, pred[32,4]{1,0:T(8,128)(4,1)S(1)} %copy.108), kind=kLoop, calls=%fused_computation.3 | loop fusion | flops 3145728 | bytes 12583040 | tf_op jit(solution)/shard_map/jit(_take)/select_n | solution.py:84
  27.7 7.7 %all-to-all-start = ((bf16[32,4,2,12,1024]{4,2,3,1,0:T(2,128)(2,1)}), bf16[32,4,2,12,1024]{4,2,3,1,0:T(2,128)(2,1)}, u32[]{:S(2)}, u32[]{:S(2)}) async-start(bf16[32,4,2,12,1024]{4,2,3,1,0:T(2,128)(2,1)} %broadcast_select_fusion), calls=%async_computation | async-start | bytes 12582912 | tf_op jit(solution)/shard_map/all_to_all | solution.py:85
  35.5 0.0 copy-done.7
  35.5 0.2 dynamic-slice_reduce_fusion
  35.7 0.0 copy-done.8
  35.7 0.1 compare_convert_fusion
  35.7 1.2 reduce-window.6
  36.9 0.1 slice.28
  37.0 0.1 copy.104
  37.2 0.1 copy.105
  37.3 0.1 add_bitcast_fusion
  37.3 0.1 fusion.24
  37.4 0.0 copy-done.6
  37.4 3.0 scatter_custom_fusion
  40.4 82.6 %all-to-all-done = bf16[32,4,2,12,1024]{4,2,3,1,0:T(2,128)(2,1)} async-done(((bf16[32,4,2,12,1024]{4,2,3,1,0:T(2,128)(2,1)}), bf16[32,4,2,12,1024]{4,2,3,1,0:T(2,128)(2,1)}, u32[]{:S(2)}, u32[]{:S(2)}) %all-to-all-start) | async-done | bytes 6291488 | tf_op jit(solution)/shard_map/all_to_all | solution.py:85
  123.0 6.4 %copy.109 = bf16[1,4,2,32,12,1024]{5,2,4,3,1,0:T(2,128)(2,1)S(1)} copy(bf16[1,4,2,32,12,1024]{5,2,4,1,3,0:T(2,128)(2,1)} %bitcast.11) | data formatting | bytes 12582912 | tf_op jit(solution)/shard_map/all_to_all | solution.py:85
  129.4 0.0 copy-start.3
  129.4 9.8 %fusion.34 = (bf16[1,4,1,384,1024]{4,2,3,1,0:T(2,128)(2,1)S(1)}, bf16[1,4,1,384,1024]{4,2,3,1,0:T(2,128)(2,1)}) fusion(bf16[1,4,2,384,1024]{4,2,3,1,0:T(2,128)(2,1)S(1)} %bitcast.62), kind=kLoop, calls=%fused_computation.73 | loop fusion | bytes 12582912 | tf_op jit(solution)/shard_map/slice | solution.py:86
  139.3 0.0 copy-done.3
  139.3 1.2 fusion
  140.5 0.0 copy-start.2
  140.5 1.3 copy-done.2
  141.8 2.7 convert_bitcast_fusion
  144.5 8.3 %convert_bitcast_fusion.1 = bf16[1,1,4,1,384,1024]{5,4,2,3,1,0:T(8,128)(2,1)} fusion(f32[4,128,1024]{2,1,0:T(8,128)} %copy-done.2, bf16[1,4,1,384,1024]{4,2,3,1,0:T(2,128)(2,1)} %get-tuple-element.35, bf16[4,128,768]{2,1,0:T(8,128)(2,1)} %bitcast.72), kind=kOutput, calls=%fused_computation.9 | convolution fusion | flops 816840704 | bytes 9175040 | tf_op jit(solution)/shard_map/kcs,kcw->ksw/dot_general | solution.py:98
  152.9 6.1 %pad_maximum_fusion = bf16[1,1,4,2,384,1024]{5,4,2,3,1,0:T(8,128)(2,1)} fusion(bf16[1,1,4,1,384,1024]{5,4,2,3,1,0:T(8,128)(2,1)} %convert_bitcast_fusion, bf16[1,1,4,1,384,1024]{5,4,2,3,1,0:T(8,128)(2,1)} %convert_bitcast_fusion.1), kind=kLoop, calls=%fused_computation.4 | loop fusion | flops 3145728 | bytes 12582912 | tf_op jit(solution)/shard_map/stack | solution.py:100
  158.9 10.9 %copy.117 = bf16[1,1,4,2,384,1024]{4,2,3,1,0,5:T(4,128)(2,1)} copy(bf16[1,1,4,2,384,1024]{5,4,2,3,1,0:T(8,128)(2,1)} %pad_maximum_fusion) | data formatting | bytes 12582912 | tf_op jit(solution)/shard_map/stack | solution.py:100
  169.8 149.4 %all_to_all.56 = bf16[1,1,4,2,384,1024]{4,2,3,1,0,5:T(4,128)(2,1)} all-to-all(bf16[1,1,4,2,384,1024]{4,2,3,1,0,5:T(4,128)(2,1)} %copy.117), channel_id=1, replica_groups=mesh['dp'=8,'own'=32] {'dp'}, dimensions={5} | all-to-all | bytes 12582912 | tf_op jit(solution)/shard_map/all_to_all | solution.py:102
  319.3 12.3 %copy.118 = bf16[1,1,4,2,384,8,128]{6,5,3,2,4,1,0:T(8,128)(2,1)} copy(bf16[1,1,4,2,384,8,128]{4,2,3,6,5,1,0:T(4,128)(2,1)} %bitcast.66) | data formatting | bytes 12582912 | tf_op jit(solution)/shard_map/all_to_all | solution.py:102
  331.6 5.0 all-to-all-start.2
  336.6 0.1 eq.65
  336.7 0.3 constant_dynamic-slice_fusion.1
  337.0 87.5 %all-to-all-done.2 = bf16[8,1,4,2,384,128]{5,0,3,2,1,4:T(8,128)(2,1)} async-done(((bf16[8,1,4,2,384,128]{5,0,3,2,1,4:T(8,128)(2,1)}), bf16[8,1,4,2,384,128]{5,0,3,2,1,4:T(8,128)(2,1)}, u32[]{:S(2)}, u32[]{:S(2)}) %all-to-all-start.2) | async-done | bytes 6291488 | tf_op jit(solution)/shard_map/all_to_all | solution.py:101
  424.5 3.9 copy.119
  428.5 5.6 copy.120
  434.0 12.1 %reshape.155 = bf16[1024,3072]{1,0:T(8,128)(2,1)} reshape(bf16[8,32,1,4,2,12,128]{6,5,4,3,1,0,2:T(8,128)(2,1)} %copy.120) | data formatting | bytes 12582912 | tf_op jit(solution)/shard_map/reshape | solution.py:50
  446.1 8.8 %copy.121 = bf16[3072,1024]{1,0:T(8,128)(2,1)} copy(bf16[3072,1024]{0,1:T(8,128)(2,1)} %bitcast.68) | data formatting | bytes 12582912 | tf_op jit(solution)/shard_map/dot_general | solution.py:51
  454.9 0.0 copy-done.4
  454.9 0.0 copy-done.5
  454.9 6.6 %constant_dynamic-update-slice_fusion.7 = (bf16[64,2,12,1024]{3,0,2,1:T(8,128)(2,1)}, bf16[64,2,12,128]{3,0,2,1:T(8,128)(2,1)S(1)}, f32[64,2,12,128]{3,0,2,1:T(8,128)}, f32[64,2,12,128]{3,0,2,1:T(8,128)}) fusion(bf16[64,2,12,128]{3,1,2,0:T(2,128)(2,1)S(1)} %constant_dynamic-slice_fusion.1, f32[64,2,12,128]{3,1,2,0:T(2,128)S(1)} %copy-done.4, ...), kind=kOutput, calls=%fused_computation.49 | convolution fusion | flops 405471232 | bytes 10620928 | tf_op jit(solution)/shard_map/dot_general | solution.py:51
  461.5 0.8 constant_dynamic-update-slice_fusion.6
  462.3 0.8 constant_dynamic-update-slice_fusion.5
  463.1 0.8 constant_dynamic-update-slice_fusion.4
  463.8 0.8 constant_dynamic-update-slice_fusion.3
  464.6 0.8 constant_dynamic-update-slice_fusion.2
  465.4 0.8 constant_dynamic-update-slice_fusion.1
  466.1 0.8 constant_dynamic-update-slice_fusion
  466.9 15.9 %copy.123 = bf16[64,2,12,1024]{0,1,2,3:T(2,128)(2,1)} copy(bf16[64,2,12,1024]{3,0,2,1:T(8,128)(2,1)} %constant_dynamic-update-slice_fusion) | data formatting | bytes 6291456 | tf_op jit(solution)/shard_map/concatenate | solution.py:115
  482.8 8.9 %reshape.184 = bf16[8,2,98304]{2,1,0:T(2,128)(2,1)} reshape(bf16[1024,12,2,64]{3,2,1,0:T(2,128)(2,1)} %bitcast.69) | data formatting | bytes 6291456
  491.7 3.7 all-to-all-start.3
  495.4 4.9 convolution_convert_fusion
  500.3 1.8 gather_fusion.1
  502.1 2.6 copy.125
  504.8 2.6 copy.126
  507.4 61.7 %all-to-all-done.3 = bf16[8,2,98304]{2,1,0:T(2,128)(2,1)S(1)} async-done(((bf16[8,2,98304]{2,1,0:T(2,128)(2,1)}), bf16[8,2,98304]{2,1,0:T(2,128)(2,1)S(1)}, u32[]{:S(2)}, u32[]{:S(2)}) %all-to-all-start.3) | async-done | bytes 3145760 | tf_op jit(solution)/shard_map/all_to_all | solution.py:116
  569.1 6.2 %reshape.185 = bf16[1024,12,2,64]{3,2,1,0:T(2,128)(2,1)} reshape(bf16[8,2,98304]{2,1,0:T(2,128)(2,1)S(1)} %all-to-all-done.3) | data formatting | bytes 6291456
  575.4 16.3 %copy.124 = bf16[64,2,12,1024]{3,1,2,0:T(2,128)(2,1)} copy(bf16[64,2,12,1024]{0,1,2,3:T(2,128)(2,1)} %bitcast.70) | data formatting | bytes 6291456
  (16 shorter events, 0.1 us)
Async XLA Ops:
  0.6 1.9 copy-start
  27.7 7.8 %copy-start.7 = (s32[256,4]{0,1:T(4,128)S(1)}, s32[256,4]{0,1:T(4,128)}, u32[]{:S(2)}) copy-start(s32[256,4]{0,1:T(4,128)} %param.11) | copy-start | bytes 12292
  27.7 7.9 %copy-start.8 = (s32[256]{0:T(256)S(1)}, s32[256]{0:T(256)}, u32[]{:S(2)}) copy-start(s32[256]{0:T(256)} %param.10) | copy-start | bytes 3076
  27.7 9.7 %copy-start.6 = (bf16[256,384]{1,0:T(8,128)(2,1)S(1)}, bf16[256,384]{1,0:T(8,128)(2,1)}, u32[]{:S(2)}) copy-start(bf16[256,384]{1,0:T(8,128)(2,1)} %param.9) | copy-start | bytes 589828
  27.7 95.3 %all-to-all-start = ((bf16[32,4,2,12,1024]{4,2,3,1,0:T(2,128)(2,1)}), bf16[32,4,2,12,1024]{4,2,3,1,0:T(2,128)(2,1)}, u32[]{:S(2)}, u32[]{:S(2)}) async-start(bf16[32,4,2,12,1024]{4,2,3,1,0:T(2,128)(2,1)} %broadcast_select_fusion), calls=%async_computation | async-start | bytes 12582912 | tf_op jit(solution)/shard_map/all_to_all | solution.py:85
  129.4 9.8 %copy-start.3 = (bf16[512,768]{1,0:T(8,128)(2,1)S(1)}, bf16[512,768]{1,0:T(8,128)(2,1)}, u32[]{:S(2)}) copy-start(bf16[512,768]{1,0:T(8,128)(2,1)} %scatter_custom_fusion) | copy-start | bytes 2359300
  140.5 1.3 copy-start.2
  331.6 92.9 %all-to-all-start.2 = ((bf16[8,1,4,2,384,128]{5,0,3,2,1,4:T(8,128)(2,1)}), bf16[8,1,4,2,384,128]{5,0,3,2,1,4:T(8,128)(2,1)}, u32[]{:S(2)}, u32[]{:S(2)}) async-start(bf16[8,1,4,2,384,128]{5,0,3,2,1,4:T(8,128)(2,1)} %bitcast.64), calls=%async_computation.2 | async-start | bytes 12582912 | tf_op jit(solution)/shard_map/all_to_all | solution.py:101
  446.1 8.8 %copy-start.4 = (f32[64,2,12,128]{3,1,2,0:T(2,128)S(1)}, f32[64,2,12,128]{3,1,2,0:T(2,128)}, u32[]{:S(2)}) copy-start(f32[64,2,12,128]{3,1,2,0:T(2,128)} %param.14) | copy-start | bytes 2359300
  446.1 8.8 %copy-start.5 = (f32[64,2,12,128]{3,1,2,0:T(2,128)S(1)}, f32[64,2,12,128]{3,1,2,0:T(2,128)}, u32[]{:S(2)}) copy-start(f32[64,2,12,128]{3,1,2,0:T(2,128)} %param.15) | copy-start | bytes 2359300
  491.7 77.4 %all-to-all-start.3 = ((bf16[8,2,98304]{2,1,0:T(2,128)(2,1)}), bf16[8,2,98304]{2,1,0:T(2,128)(2,1)S(1)}, u32[]{:S(2)}, u32[]{:S(2)}) async-start(bf16[8,2,98304]{2,1,0:T(2,128)(2,1)} %reshape.184), calls=%async_computation.3 | async-start | bytes 6291456 | tf_op jit(solution)/shard_map/all_to_all | solution.py:116
  575.4 16.3 %copy-start.1 = (bf16[64,2,12,1024]{3,1,2,0:T(2,128)(2,1)S(1)}, bf16[64,2,12,1024]{3,1,2,0:T(2,128)(2,1)}, u32[]{:S(2)}) copy-start(bf16[64,2,12,1024]{3,1,2,0:T(2,128)(2,1)} %param.13) | copy-start | bytes 9437188
